TPU v7x, 512 devices: a whole 4x8x8 slice. The times are simulated.
512 devices in a mesh: band: 4 (over x), tile: 16 (over y_lo, z), slab: 8 (over y_hi, core).
Axes of the slice: x: 4, y: 8 (y_hi: 4, y_lo: 2; y = y_hi * 2 + y_lo), z: 8, core: 2. Of those that a mesh axis runs over, the one named last changes fastest.
Arguments:
- strength: float32 [32], P('band'), may hold values from 0.0005 to 0.5
- opacity: float32 [64, 256, 256], P('slab', 'tile'), may hold values from 0.5 to 2
- planck: float32 [64, 256, 256], P('slab', 'tile'), may hold values from 0.5 to 2
- old_populations: float32 [5, 64, 256, 256], P(None, 'slab', 'tile'), may hold values from 0.1 to 1
- line_index: int32 [32], P('band'), may hold values from 0 to 4
- line_weight: float32 [32], P('band'), may hold values from 0.2 to 1
Outputs:
- new_populations: float32 [5, 64, 256, 256], P(None, 'slab', 'tile', 'band')
- new_source: float32 [32, 64, 256, 256], P('band', 'slab', 'tile')
Inputs may be any that keep to these rules, and one draw needn't show every extreme that they name: line_index names a transition of the model atom.
All inputs are finite; a program needn't handle non-finite values.
Results may differ from a plain program's by a relative error of at most 0.0001.
Values sent between devices are 32-bit elements; how exact they have to be, the bound alone decides.
No kernel may reach another device: no remote copies, remote signals or barrier semaphores. Data moves between devices by JAX's collectives and lax.ppermute only.
A program may use at most 64 MiB of HBM per device.

v0:
```python
import jax
import jax.numpy as jnp
from jax import lax
from jax.sharding import PartitionSpec as P

LINES = 5
EPS_THERMAL = 0.1
COLLISION = 0.5
PATH_FACTOR = 1.25
TILT_SHARE = 0.4
LOWER_LEVEL = (0, 0, 1, 1, 2)
UPPER_LEVEL = (3, 4, 3, 4, 4)


def extended_2(cells, sides, width):
    for axis, dim in sides:
        count = lax.axis_size(axis)
        ends = count - 1
        head = lax.slice_in_dim(cells, 0, width, axis=dim)
        tail = lax.slice_in_dim(cells, cells.shape[dim] - width, cells.shape[dim], axis=dim)
        cells = jnp.concatenate(
            [
                lax.ppermute(tail, axis, [(i, (i + 1) % count) for i in range(ends)]),
                cells,
                lax.ppermute(head, axis, [((i + 1) % count, i) for i in range(ends)]),
            ],
            axis=dim,
        )
    return cells


def shifted(block, axis, distance):
    devices = range(lax.axis_size(axis))
    route = [(i - distance, i) for i in devices if i - distance in devices]
    return lax.ppermute(block, axis, route)


def relax(jbar, planck):
    ratios = (jbar + COLLISION * planck[None]) / (1.0 + jbar + COLLISION)
    ground = jnp.ones_like(planck)
    level_three = ratios[0]
    level_four = ratios[1]
    level_one = 0.5 * (level_three / ratios[2] + level_four / ratios[3])
    level_two = level_four / ratios[4]
    stacked = jnp.stack([ground, level_one, level_two, level_three, level_four], axis=0)
    return stacked / jnp.sum(stacked, axis=0)


def line_sources(levels_now):
    return jnp.stack(
        [
            levels_now[UPPER_LEVEL[t]] / (levels_now[LOWER_LEVEL[t]] + levels_now[UPPER_LEVEL[t]])
            for t in range(5)
        ],
        axis=0,
    )


def sweep(face_ext, strength, opacity_ext, source_ext, margin):
    intensity = face_ext
    layer_sums = []
    for plane in range(opacity_ext.shape[0]):
        attenuation = jnp.exp(-PATH_FACTOR * strength[:, None, None] * opacity_ext[plane][None])[
            :, None
        ]
        zero_column = jnp.zeros_like(intensity[:, 0, :1])
        from_left = jnp.concatenate([zero_column, intensity[:, 0, :-1]], axis=1)
        from_right = jnp.concatenate([intensity[:, 1, 1:], zero_column], axis=1)
        upwind = jnp.stack([from_left, from_right], axis=1)
        intensity = (
            attenuation * ((1.0 - TILT_SHARE) * intensity + TILT_SHARE * upwind)
            + (1.0 - attenuation) * source_ext[:, plane][:, None]
        )
        layer_sums.append(jnp.sum(intensity[:, :, margin:-margin], axis=1))
    return (intensity[:, :, margin:-margin], jnp.stack(layer_sums, axis=1))


def per_device(strength, opacity, planck, old_populations, line_index, line_weight):
    highest = lax.Precision.HIGHEST
    slab_depth, tile_rows, cells_y = opacity.shape
    freq_count = strength.shape[0]
    total_freqs = freq_count * lax.axis_size("band")
    onehot = (line_index[:, None] == jnp.arange(LINES, dtype=jnp.int32)[None, :]).astype(
        jnp.float32
    )
    weighted = onehot * line_weight[:, None] * (LINES / (2.0 * total_freqs))
    fields = jnp.concatenate([opacity[None], planck[None], old_populations], axis=0)
    fields_ext = extended_2(fields, (("tile", 2),), slab_depth)
    opacity_ext = fields_ext[0]
    planck_ext = fields_ext[1]
    levels_ext = fields_ext[2:]
    extended = tile_rows + 2 * slab_depth
    global_x = (
        lax.axis_index("tile") * tile_rows - slab_depth + jnp.arange(extended, dtype=jnp.int32)
    )
    inside = ((global_x >= 0) & (global_x < tile_rows * lax.axis_size("tile")))[None, :, None]
    lower_ext = jnp.stack([levels_ext[LOWER_LEVEL[t]] for t in range(5)], axis=0)
    upper_ext = jnp.stack([levels_ext[UPPER_LEVEL[t]] for t in range(5)], axis=0)
    denominator = jnp.where(inside, lower_ext + upper_ext, 1.0)
    line_ext = jnp.where(inside, upper_ext / denominator, 0.0)
    source_ext = jnp.where(
        inside,
        EPS_THERMAL * planck_ext[None]
        + (1.0 - EPS_THERMAL) * jnp.einsum("ft,tzxy->fzxy", onehot, line_ext, precision=highest),
        0.0,
    )
    slab_count = lax.axis_size("slab")

    def whole_step(step, carry):
        face_in, previous = carry
        face_ext = extended_2(face_in, (("tile", 2),), slab_depth)
        bottom, layer_sums = sweep(face_ext, strength, opacity_ext, source_ext, slab_depth)
        return (shifted(bottom, "slab", 1), layer_sums)

    face_start = jnp.zeros((freq_count, 2, tile_rows, cells_y), jnp.float32)
    initial = (face_start, jnp.zeros((freq_count, slab_depth, tile_rows, cells_y), jnp.float32))
    _, layer_sums = lax.fori_loop(0, slab_count, whole_step, initial)
    jbar = jnp.einsum("ft,fzxy->tzxy", weighted, layer_sums, precision=highest)
    share = cells_y // lax.axis_size("band")
    offset = lax.axis_index("band") * share
    jbar_share = lax.psum_scatter(jbar, "band", scatter_dimension=3, tiled=True)
    planck_share = lax.dynamic_slice_in_dim(planck, offset, share, 2)
    populations_share = relax(jbar_share, planck_share)
    populations_all = lax.all_gather(populations_share, "band", axis=3, tiled=True)
    new_source = EPS_THERMAL * planck[None] + (1.0 - EPS_THERMAL) * jnp.einsum(
        "ft,tzxy->fzxy", onehot, line_sources(populations_all), precision=highest
    )
    return (populations_share, new_source)


def solution(mesh):
    in_specs = (
        P("band"),
        P("slab", "tile", None),
        P("slab", "tile", None),
        P(None, "slab", "tile", None),
        P("band"),
        P("band"),
    )
    out_specs = (P(None, "slab", "tile", "band"), P("band", "slab", "tile", None))
    return jax.shard_map(
        per_device, mesh=mesh, in_specs=in_specs, out_specs=out_specs, check_vma=False
    )
```

profile of v0, /device:TPU:8, one launch (start us, length us, event | category | flops | bytes accessed | tf_op | source)
XLA Modules:
  0.0 435.0 jit_solution(6454355539191148617)
XLA Ops:
  8.7 4.3 collective-permute-start.3
  13.0 8.5 %collective-permute-start.4 = (f32[7,8,8,256]{3,2,1,0:T(8,128)S(1)}, f32[7,8,8,256]{3,2,1,0:T(8,128)}, u32[]{:S(2)}, u32[]{:S(2)}) collective-permute-start(f32[7,8,8,256]{3,2,1,0:T(8,128)S(1)} %get-tuple-element.113), channel_id=1, source_target_pairs={{8,0},{16,8},{24,16},{32,24},{40,32},{48,40},{56,48},{64,56},{72,6... | collective-permute-start | bytes 1376264 | tf_op jit(solution)/shard_map/ppermute | solution.py:25
  21.5 8.5 %collective-permute-done.3 = f32[7,8,8,256]{3,2,1,0:T(8,128)S(1)} collective-permute-done((f32[7,8,8,256]{3,2,1,0:T(8,128)S(1)}, f32[7,8,8,256]{3,2,1,0:T(8,128)S(1)}, u32[]{:S(2)}, u32[]{:S(2)}) %collective-permute-start.3) | collective-permute-done | bytes 458784 | tf_op jit(solution)/shard_map/ppermute | solution.py:23
  37.6 251.7 %while.12 = (s32[]{:T(128)}, f32[8,2,16,256]{3,2,0,1:T(8,128)S(1)}, f32[8,8,16,256]{3,2,0,1:T(8,128)}, f32[8]{0:T(128)S(1)}, f32[8,32,256]{2,1,0:T(8,128)S(1)}, /*index=5*/f32[8,8,32,256]{3,2,0,1:T(8,128)}, s32[]{:T(128)}) while((s32[]{:T(128)}, f32[8,2,16,256]{3,2,0,1:T(8,128)S(1)}, f32[8,8,16,256]{3,2,0,1:T(8,128)}, f32[8]{0:T(128)S(1)}, ...), condition=%wide.region_9.10_spmd, body=%wide.region_0.9_spmd.sunk | while | flops 24772616 | bytes 81658408 | solution.py:117
  40.5 6.6 %collective-permute-start.1 = (f32[8,2,8,256]{3,2,0,1:T(8,128)}, f32[8,2,8,256]{3,2,0,1:T(8,128)}, u32[]{:S(2)}, u32[]{:S(2)}) collective-permute-start(f32[8,2,8,256]{3,2,0,1:T(8,128)} %get-tuple-element.218), channel_id=1, source_target_pairs={{8,0},{16,8},{24,16},{32,24},{40,32},{48,40},{56,48},{64,56},{72,6... | collective-permute-start | bytes 393224 | tf_op jit(solution)/shard_map/while/body/eval_jaxpr/ppermute | solution.py:25
  47.2 2.8 multiply_bitcast_fusion.9
  67.0 6.0 %collective-permute-start.1 = (f32[8,2,8,256]{3,2,0,1:T(8,128)}, f32[8,2,8,256]{3,2,0,1:T(8,128)}, u32[]{:S(2)}, u32[]{:S(2)}) collective-permute-start(f32[8,2,8,256]{3,2,0,1:T(8,128)} %get-tuple-element.218), channel_id=1, source_target_pairs={{8,0},{16,8},{24,16},{32,24},{40,32},{48,40},{56,48},{64,56},{72,6... | collective-permute-start | bytes 393224 | tf_op jit(solution)/shard_map/while/body/eval_jaxpr/ppermute | solution.py:25
  73.1 2.8 multiply_bitcast_fusion.9
  87.8 6.8 %collective-permute-start.2 = (f32[8,2,16,256]{3,2,0,1:T(8,128)S(1)}, f32[8,2,16,256]{3,2,0,1:T(8,128)S(1)}, u32[]{:S(2)}, u32[]{:S(2)}) collective-permute-start(f32[8,2,16,256]{3,2,0,1:T(8,128)S(1)} %get-tuple-element.252), channel_id=1, source_target_pairs={{0,1},{1,2},{2,3},{3,4},{4,5},{5,6},{6,7},{8,9},{9,10},{10,11},{11... | collective-permute-start | bytes 786440 | tf_op jit(solution)/shard_map/while/body/eval_jaxpr/ppermute | solution.py:35
  98.5 6.0 %collective-permute-start.1 = (f32[8,2,8,256]{3,2,0,1:T(8,128)}, f32[8,2,8,256]{3,2,0,1:T(8,128)}, u32[]{:S(2)}, u32[]{:S(2)}) collective-permute-start(f32[8,2,8,256]{3,2,0,1:T(8,128)} %get-tuple-element.218), channel_id=1, source_target_pairs={{8,0},{16,8},{24,16},{32,24},{40,32},{48,40},{56,48},{64,56},{72,6... | collective-permute-start | bytes 393224 | tf_op jit(solution)/shard_map/while/body/eval_jaxpr/ppermute | solution.py:25
  104.6 2.8 multiply_bitcast_fusion.9
  119.3 7.5 %collective-permute-start.2 = (f32[8,2,16,256]{3,2,0,1:T(8,128)S(1)}, f32[8,2,16,256]{3,2,0,1:T(8,128)S(1)}, u32[]{:S(2)}, u32[]{:S(2)}) collective-permute-start(f32[8,2,16,256]{3,2,0,1:T(8,128)S(1)} %get-tuple-element.252), channel_id=1, source_target_pairs={{0,1},{1,2},{2,3},{3,4},{4,5},{5,6},{6,7},{8,9},{9,10},{10,11},{11... | collective-permute-start | bytes 786440 | tf_op jit(solution)/shard_map/while/body/eval_jaxpr/ppermute | solution.py:35
  130.7 6.0 %collective-permute-start.1 = (f32[8,2,8,256]{3,2,0,1:T(8,128)}, f32[8,2,8,256]{3,2,0,1:T(8,128)}, u32[]{:S(2)}, u32[]{:S(2)}) collective-permute-start(f32[8,2,8,256]{3,2,0,1:T(8,128)} %get-tuple-element.218), channel_id=1, source_target_pairs={{8,0},{16,8},{24,16},{32,24},{40,32},{48,40},{56,48},{64,56},{72,6... | collective-permute-start | bytes 393224 | tf_op jit(solution)/shard_map/while/body/eval_jaxpr/ppermute | solution.py:25
  136.8 2.8 multiply_bitcast_fusion.9
  151.5 7.6 %collective-permute-start.2 = (f32[8,2,16,256]{3,2,0,1:T(8,128)S(1)}, f32[8,2,16,256]{3,2,0,1:T(8,128)S(1)}, u32[]{:S(2)}, u32[]{:S(2)}) collective-permute-start(f32[8,2,16,256]{3,2,0,1:T(8,128)S(1)} %get-tuple-element.252), channel_id=1, source_target_pairs={{0,1},{1,2},{2,3},{3,4},{4,5},{5,6},{6,7},{8,9},{9,10},{10,11},{11... | collective-permute-start | bytes 786440 | tf_op jit(solution)/shard_map/while/body/eval_jaxpr/ppermute | solution.py:35
  162.9 6.0 %collective-permute-start.1 = (f32[8,2,8,256]{3,2,0,1:T(8,128)}, f32[8,2,8,256]{3,2,0,1:T(8,128)}, u32[]{:S(2)}, u32[]{:S(2)}) collective-permute-start(f32[8,2,8,256]{3,2,0,1:T(8,128)} %get-tuple-element.218), channel_id=1, source_target_pairs={{8,0},{16,8},{24,16},{32,24},{40,32},{48,40},{56,48},{64,56},{72,6... | collective-permute-start | bytes 393224 | tf_op jit(solution)/shard_map/while/body/eval_jaxpr/ppermute | solution.py:25
  169.0 2.8 multiply_bitcast_fusion.9
  183.7 7.6 %collective-permute-start.2 = (f32[8,2,16,256]{3,2,0,1:T(8,128)S(1)}, f32[8,2,16,256]{3,2,0,1:T(8,128)S(1)}, u32[]{:S(2)}, u32[]{:S(2)}) collective-permute-start(f32[8,2,16,256]{3,2,0,1:T(8,128)S(1)} %get-tuple-element.252), channel_id=1, source_target_pairs={{0,1},{1,2},{2,3},{3,4},{4,5},{5,6},{6,7},{8,9},{9,10},{10,11},{11... | collective-permute-start | bytes 786440 | tf_op jit(solution)/shard_map/while/body/eval_jaxpr/ppermute | solution.py:35
  195.1 6.0 %collective-permute-start.1 = (f32[8,2,8,256]{3,2,0,1:T(8,128)}, f32[8,2,8,256]{3,2,0,1:T(8,128)}, u32[]{:S(2)}, u32[]{:S(2)}) collective-permute-start(f32[8,2,8,256]{3,2,0,1:T(8,128)} %get-tuple-element.218), channel_id=1, source_target_pairs={{8,0},{16,8},{24,16},{32,24},{40,32},{48,40},{56,48},{64,56},{72,6... | collective-permute-start | bytes 393224 | tf_op jit(solution)/shard_map/while/body/eval_jaxpr/ppermute | solution.py:25
  201.2 2.8 multiply_bitcast_fusion.9
  215.9 7.6 %collective-permute-start.2 = (f32[8,2,16,256]{3,2,0,1:T(8,128)S(1)}, f32[8,2,16,256]{3,2,0,1:T(8,128)S(1)}, u32[]{:S(2)}, u32[]{:S(2)}) collective-permute-start(f32[8,2,16,256]{3,2,0,1:T(8,128)S(1)} %get-tuple-element.252), channel_id=1, source_target_pairs={{0,1},{1,2},{2,3},{3,4},{4,5},{5,6},{6,7},{8,9},{9,10},{10,11},{11... | collective-permute-start | bytes 786440 | tf_op jit(solution)/shard_map/while/body/eval_jaxpr/ppermute | solution.py:35
  227.3 6.0 %collective-permute-start.1 = (f32[8,2,8,256]{3,2,0,1:T(8,128)}, f32[8,2,8,256]{3,2,0,1:T(8,128)}, u32[]{:S(2)}, u32[]{:S(2)}) collective-permute-start(f32[8,2,8,256]{3,2,0,1:T(8,128)} %get-tuple-element.218), channel_id=1, source_target_pairs={{8,0},{16,8},{24,16},{32,24},{40,32},{48,40},{56,48},{64,56},{72,6... | collective-permute-start | bytes 393224 | tf_op jit(solution)/shard_map/while/body/eval_jaxpr/ppermute | solution.py:25
  248.1 7.6 %collective-permute-start.2 = (f32[8,2,16,256]{3,2,0,1:T(8,128)S(1)}, f32[8,2,16,256]{3,2,0,1:T(8,128)S(1)}, u32[]{:S(2)}, u32[]{:S(2)}) collective-permute-start(f32[8,2,16,256]{3,2,0,1:T(8,128)S(1)} %get-tuple-element.252), channel_id=1, source_target_pairs={{0,1},{1,2},{2,3},{3,4},{4,5},{5,6},{6,7},{8,9},{9,10},{10,11},{11... | collective-permute-start | bytes 786440 | tf_op jit(solution)/shard_map/while/body/eval_jaxpr/ppermute | solution.py:35
  259.5 6.0 %collective-permute-start.1 = (f32[8,2,8,256]{3,2,0,1:T(8,128)}, f32[8,2,8,256]{3,2,0,1:T(8,128)}, u32[]{:S(2)}, u32[]{:S(2)}) collective-permute-start(f32[8,2,8,256]{3,2,0,1:T(8,128)} %get-tuple-element.218), channel_id=1, source_target_pairs={{8,0},{16,8},{24,16},{32,24},{40,32},{48,40},{56,48},{64,56},{72,6... | collective-permute-start | bytes 393224 | tf_op jit(solution)/shard_map/while/body/eval_jaxpr/ppermute | solution.py:25
  280.3 7.8 %collective-permute-start.2 = (f32[8,2,16,256]{3,2,0,1:T(8,128)S(1)}, f32[8,2,16,256]{3,2,0,1:T(8,128)S(1)}, u32[]{:S(2)}, u32[]{:S(2)}) collective-permute-start(f32[8,2,16,256]{3,2,0,1:T(8,128)S(1)} %get-tuple-element.252), channel_id=1, source_target_pairs={{0,1},{1,2},{2,3},{3,4},{4,5},{5,6},{6,7},{8,9},{9,10},{10,11},{11... | collective-permute-start | bytes 786440 | tf_op jit(solution)/shard_map/while/body/eval_jaxpr/ppermute | solution.py:35
  289.3 2.8 fusion.33
  292.1 13.8 %copy.27 = f32[5,8,16,256]{0,2,1,3:T(8,128)} copy(f32[5,8,16,256]{3,0,2,1:T(8,128)S(1)} %fusion.33) | data formatting | bytes 1310720
  305.9 11.9 %reshape.106 = f32[256,640]{1,0:T(8,128)} reshape(f32[256,8,16,5]{3,2,1,0:T(8,128)} %bitcast.211) | data formatting | bytes 1310720
  318.6 43.0 %reduce-scatter.4.cloned.1.call-done = f32[64,640]{1,0:T(8,128)} async-done(((f32[256,640]{1,0:T(8,128)}), f32[64,640]{1,0:T(8,128)}) %reduce-scatter.4.cloned.1.call-update) | async-done | bytes 163856
  361.5 6.2 %reshape.107 = f32[64,8,16,5]{3,2,1,0:T(8,128)} reshape(f32[64,640]{1,0:T(8,128)} %reduce-scatter.4.cloned.1.call-done) | data formatting | bytes 327680
  367.8 3.8 copy.28
  373.9 45.2 %all_gather.3 = f32[5,8,16,256]{2,1,0,3:T(8,128)S(1)} all-gather(f32[5,8,16,64]{2,1,0,3:T(8,128)S(1)} %copy.14), channel_id=1, replica_groups=mesh['band'=4,'tile'=16,'slab'=8] {'band'}, dimensions={3}, use_global_device_ids=true | all-gather | bytes 819200 | tf_op jit(solution)/shard_map/all_gather | solution.py:124
  (646 shorter events, 151.2 us)
Async XLA Ops:
  7.2 354.4 %reduce-scatter.4.cloned.1.call-start = ((), (), s32[]{:S(2)}) async-start(), calls=%async_computation.1 | async-start | bytes 819200
  7.2 24.0 %copy-start.7 = (f32[5,8,16,256]{3,2,1,0:T(8,128)S(1)}, f32[5,8,16,256]{3,2,1,0:T(8,128)}, u32[]{:S(2)}) copy-start(f32[5,8,16,256]{3,2,1,0:T(8,128)} %param.11) | copy-start | bytes 1966084
  7.2 24.0 %copy-start.8 = (f32[8,16,256]{2,1,0:T(8,128)S(1)}, f32[8,16,256]{2,1,0:T(8,128)}, u32[]{:S(2)}) copy-start(f32[8,16,256]{2,1,0:T(8,128)} %param.10) | copy-start | bytes 393220
  7.2 24.0 %copy-start.11 = (f32[8,16,256]{2,1,0:T(8,128)S(1)}, f32[8,16,256]{2,1,0:T(8,128)}, u32[]{:S(2)}) copy-start(f32[8,16,256]{2,1,0:T(8,128)} %param.9) | copy-start | bytes 393220
  8.7 21.3 %collective-permute-start.3 = (f32[7,8,8,256]{3,2,1,0:T(8,128)S(1)}, f32[7,8,8,256]{3,2,1,0:T(8,128)S(1)}, u32[]{:S(2)}, u32[]{:S(2)}) collective-permute-start(f32[7,8,8,256]{3,2,1,0:T(8,128)S(1)} %get-tuple-element.112), channel_id=1, source_target_pairs={{0,8},{8,16},{16,24},{24,32},{32,40},{40,48},{48,56},{56,64},{64,7... | collective-permute-start | bytes 1376264 | tf_op jit(solution)/shard_map/ppermute | solution.py:23
  13.0 18.2 %collective-permute-start.4 = (f32[7,8,8,256]{3,2,1,0:T(8,128)S(1)}, f32[7,8,8,256]{3,2,1,0:T(8,128)}, u32[]{:S(2)}, u32[]{:S(2)}) collective-permute-start(f32[7,8,8,256]{3,2,1,0:T(8,128)S(1)} %get-tuple-element.113), channel_id=1, source_target_pairs={{8,0},{16,8},{24,16},{32,24},{40,32},{48,40},{56,48},{64,56},{72,6... | collective-permute-start | bytes 1376264 | tf_op jit(solution)/shard_map/ppermute | solution.py:25
  37.5 251.7 %copy-start.15 = (f32[8]{0:T(128)S(1)}, f32[8]{0:T(128)}, u32[]{:S(2)}) copy-start(f32[8]{0:T(128)} %param.13) | copy-start | bytes 100
  38.6 13.2 %collective-permute-start = (f32[8,2,8,256]{3,2,0,1:T(8,128)}, f32[8,2,8,256]{3,2,0,1:T(8,128)}, u32[]{:S(2)}, u32[]{:S(2)}) collective-permute-start(f32[8,2,8,256]{3,2,0,1:T(8,128)} %get-tuple-element.217), channel_id=1, source_target_pairs={{0,8},{8,16},{16,24},{24,32},{32,40},{40,48},{48,56},{56,64},{64,7... | collective-permute-start | bytes 393224 | tf_op jit(solution)/shard_map/while/body/eval_jaxpr/ppermute | solution.py:23
  40.5 13.1 %collective-permute-start.1 = (f32[8,2,8,256]{3,2,0,1:T(8,128)}, f32[8,2,8,256]{3,2,0,1:T(8,128)}, u32[]{:S(2)}, u32[]{:S(2)}) collective-permute-start(f32[8,2,8,256]{3,2,0,1:T(8,128)} %get-tuple-element.218), channel_id=1, source_target_pairs={{8,0},{16,8},{24,16},{32,24},{40,32},{48,40},{56,48},{64,56},{72,6... | collective-permute-start | bytes 393224 | tf_op jit(solution)/shard_map/while/body/eval_jaxpr/ppermute | solution.py:25
  61.9 2.4 collective-permute-start.2
  65.1 12.6 %collective-permute-start = (f32[8,2,8,256]{3,2,0,1:T(8,128)}, f32[8,2,8,256]{3,2,0,1:T(8,128)}, u32[]{:S(2)}, u32[]{:S(2)}) collective-permute-start(f32[8,2,8,256]{3,2,0,1:T(8,128)} %get-tuple-element.217), channel_id=1, source_target_pairs={{0,8},{8,16},{16,24},{24,32},{32,40},{40,48},{48,56},{56,64},{64,7... | collective-permute-start | bytes 393224 | tf_op jit(solution)/shard_map/while/body/eval_jaxpr/ppermute | solution.py:23
  67.0 12.6 %collective-permute-start.1 = (f32[8,2,8,256]{3,2,0,1:T(8,128)}, f32[8,2,8,256]{3,2,0,1:T(8,128)}, u32[]{:S(2)}, u32[]{:S(2)}) collective-permute-start(f32[8,2,8,256]{3,2,0,1:T(8,128)} %get-tuple-element.218), channel_id=1, source_target_pairs={{8,0},{16,8},{24,16},{32,24},{40,32},{48,40},{56,48},{64,56},{72,6... | collective-permute-start | bytes 393224 | tf_op jit(solution)/shard_map/while/body/eval_jaxpr/ppermute | solution.py:25
  87.8 8.0 %collective-permute-start.2 = (f32[8,2,16,256]{3,2,0,1:T(8,128)S(1)}, f32[8,2,16,256]{3,2,0,1:T(8,128)S(1)}, u32[]{:S(2)}, u32[]{:S(2)}) collective-permute-start(f32[8,2,16,256]{3,2,0,1:T(8,128)S(1)} %get-tuple-element.252), channel_id=1, source_target_pairs={{0,1},{1,2},{2,3},{3,4},{4,5},{5,6},{6,7},{8,9},{9,10},{10,11},{11... | collective-permute-start | bytes 786440 | tf_op jit(solution)/shard_map/while/body/eval_jaxpr/ppermute | solution.py:35
  96.6 12.6 %collective-permute-start = (f32[8,2,8,256]{3,2,0,1:T(8,128)}, f32[8,2,8,256]{3,2,0,1:T(8,128)}, u32[]{:S(2)}, u32[]{:S(2)}) collective-permute-start(f32[8,2,8,256]{3,2,0,1:T(8,128)} %get-tuple-element.217), channel_id=1, source_target_pairs={{0,8},{8,16},{16,24},{24,32},{32,40},{40,48},{48,56},{56,64},{64,7... | collective-permute-start | bytes 393224 | tf_op jit(solution)/shard_map/while/body/eval_jaxpr/ppermute | solution.py:23
  98.5 12.6 %collective-permute-start.1 = (f32[8,2,8,256]{3,2,0,1:T(8,128)}, f32[8,2,8,256]{3,2,0,1:T(8,128)}, u32[]{:S(2)}, u32[]{:S(2)}) collective-permute-start(f32[8,2,8,256]{3,2,0,1:T(8,128)} %get-tuple-element.218), channel_id=1, source_target_pairs={{8,0},{16,8},{24,16},{32,24},{40,32},{48,40},{56,48},{64,56},{72,6... | collective-permute-start | bytes 393224 | tf_op jit(solution)/shard_map/while/body/eval_jaxpr/ppermute | solution.py:25
  119.3 8.6 %collective-permute-start.2 = (f32[8,2,16,256]{3,2,0,1:T(8,128)S(1)}, f32[8,2,16,256]{3,2,0,1:T(8,128)S(1)}, u32[]{:S(2)}, u32[]{:S(2)}) collective-permute-start(f32[8,2,16,256]{3,2,0,1:T(8,128)S(1)} %get-tuple-element.252), channel_id=1, source_target_pairs={{0,1},{1,2},{2,3},{3,4},{4,5},{5,6},{6,7},{8,9},{9,10},{10,11},{11... | collective-permute-start | bytes 786440 | tf_op jit(solution)/shard_map/while/body/eval_jaxpr/ppermute | solution.py:35
  128.7 12.6 %collective-permute-start = (f32[8,2,8,256]{3,2,0,1:T(8,128)}, f32[8,2,8,256]{3,2,0,1:T(8,128)}, u32[]{:S(2)}, u32[]{:S(2)}) collective-permute-start(f32[8,2,8,256]{3,2,0,1:T(8,128)} %get-tuple-element.217), channel_id=1, source_target_pairs={{0,8},{8,16},{16,24},{24,32},{32,40},{40,48},{48,56},{56,64},{64,7... | collective-permute-start | bytes 393224 | tf_op jit(solution)/shard_map/while/body/eval_jaxpr/ppermute | solution.py:23
  130.7 12.6 %collective-permute-start.1 = (f32[8,2,8,256]{3,2,0,1:T(8,128)}, f32[8,2,8,256]{3,2,0,1:T(8,128)}, u32[]{:S(2)}, u32[]{:S(2)}) collective-permute-start(f32[8,2,8,256]{3,2,0,1:T(8,128)} %get-tuple-element.218), channel_id=1, source_target_pairs={{8,0},{16,8},{24,16},{32,24},{40,32},{48,40},{56,48},{64,56},{72,6... | collective-permute-start | bytes 393224 | tf_op jit(solution)/shard_map/while/body/eval_jaxpr/ppermute | solution.py:25
  151.5 8.7 %collective-permute-start.2 = (f32[8,2,16,256]{3,2,0,1:T(8,128)S(1)}, f32[8,2,16,256]{3,2,0,1:T(8,128)S(1)}, u32[]{:S(2)}, u32[]{:S(2)}) collective-permute-start(f32[8,2,16,256]{3,2,0,1:T(8,128)S(1)} %get-tuple-element.252), channel_id=1, source_target_pairs={{0,1},{1,2},{2,3},{3,4},{4,5},{5,6},{6,7},{8,9},{9,10},{10,11},{11... | collective-permute-start | bytes 786440 | tf_op jit(solution)/shard_map/while/body/eval_jaxpr/ppermute | solution.py:35
  160.9 12.6 %collective-permute-start = (f32[8,2,8,256]{3,2,0,1:T(8,128)}, f32[8,2,8,256]{3,2,0,1:T(8,128)}, u32[]{:S(2)}, u32[]{:S(2)}) collective-permute-start(f32[8,2,8,256]{3,2,0,1:T(8,128)} %get-tuple-element.217), channel_id=1, source_target_pairs={{0,8},{8,16},{16,24},{24,32},{32,40},{40,48},{48,56},{56,64},{64,7... | collective-permute-start | bytes 393224 | tf_op jit(solution)/shard_map/while/body/eval_jaxpr/ppermute | solution.py:23
  162.9 12.6 %collective-permute-start.1 = (f32[8,2,8,256]{3,2,0,1:T(8,128)}, f32[8,2,8,256]{3,2,0,1:T(8,128)}, u32[]{:S(2)}, u32[]{:S(2)}) collective-permute-start(f32[8,2,8,256]{3,2,0,1:T(8,128)} %get-tuple-element.218), channel_id=1, source_target_pairs={{8,0},{16,8},{24,16},{32,24},{40,32},{48,40},{56,48},{64,56},{72,6... | collective-permute-start | bytes 393224 | tf_op jit(solution)/shard_map/while/body/eval_jaxpr/ppermute | solution.py:25
  183.7 8.7 %collective-permute-start.2 = (f32[8,2,16,256]{3,2,0,1:T(8,128)S(1)}, f32[8,2,16,256]{3,2,0,1:T(8,128)S(1)}, u32[]{:S(2)}, u32[]{:S(2)}) collective-permute-start(f32[8,2,16,256]{3,2,0,1:T(8,128)S(1)} %get-tuple-element.252), channel_id=1, source_target_pairs={{0,1},{1,2},{2,3},{3,4},{4,5},{5,6},{6,7},{8,9},{9,10},{10,11},{11... | collective-permute-start | bytes 786440 | tf_op jit(solution)/shard_map/while/body/eval_jaxpr/ppermute | solution.py:35
  193.2 12.6 %collective-permute-start = (f32[8,2,8,256]{3,2,0,1:T(8,128)}, f32[8,2,8,256]{3,2,0,1:T(8,128)}, u32[]{:S(2)}, u32[]{:S(2)}) collective-permute-start(f32[8,2,8,256]{3,2,0,1:T(8,128)} %get-tuple-element.217), channel_id=1, source_target_pairs={{0,8},{8,16},{16,24},{24,32},{32,40},{40,48},{48,56},{56,64},{64,7... | collective-permute-start | bytes 393224 | tf_op jit(solution)/shard_map/while/body/eval_jaxpr/ppermute | solution.py:23
  195.1 12.6 %collective-permute-start.1 = (f32[8,2,8,256]{3,2,0,1:T(8,128)}, f32[8,2,8,256]{3,2,0,1:T(8,128)}, u32[]{:S(2)}, u32[]{:S(2)}) collective-permute-start(f32[8,2,8,256]{3,2,0,1:T(8,128)} %get-tuple-element.218), channel_id=1, source_target_pairs={{8,0},{16,8},{24,16},{32,24},{40,32},{48,40},{56,48},{64,56},{72,6... | collective-permute-start | bytes 393224 | tf_op jit(solution)/shard_map/while/body/eval_jaxpr/ppermute | solution.py:25
  215.9 8.7 %collective-permute-start.2 = (f32[8,2,16,256]{3,2,0,1:T(8,128)S(1)}, f32[8,2,16,256]{3,2,0,1:T(8,128)S(1)}, u32[]{:S(2)}, u32[]{:S(2)}) collective-permute-start(f32[8,2,16,256]{3,2,0,1:T(8,128)S(1)} %get-tuple-element.252), channel_id=1, source_target_pairs={{0,1},{1,2},{2,3},{3,4},{4,5},{5,6},{6,7},{8,9},{9,10},{10,11},{11... | collective-permute-start | bytes 786440 | tf_op jit(solution)/shard_map/while/body/eval_jaxpr/ppermute | solution.py:35
  225.4 12.6 %collective-permute-start = (f32[8,2,8,256]{3,2,0,1:T(8,128)}, f32[8,2,8,256]{3,2,0,1:T(8,128)}, u32[]{:S(2)}, u32[]{:S(2)}) collective-permute-start(f32[8,2,8,256]{3,2,0,1:T(8,128)} %get-tuple-element.217), channel_id=1, source_target_pairs={{0,8},{8,16},{16,24},{24,32},{32,40},{40,48},{48,56},{56,64},{64,7... | collective-permute-start | bytes 393224 | tf_op jit(solution)/shard_map/while/body/eval_jaxpr/ppermute | solution.py:23
  227.3 12.6 %collective-permute-start.1 = (f32[8,2,8,256]{3,2,0,1:T(8,128)}, f32[8,2,8,256]{3,2,0,1:T(8,128)}, u32[]{:S(2)}, u32[]{:S(2)}) collective-permute-start(f32[8,2,8,256]{3,2,0,1:T(8,128)} %get-tuple-element.218), channel_id=1, source_target_pairs={{8,0},{16,8},{24,16},{32,24},{40,32},{48,40},{56,48},{64,56},{72,6... | collective-permute-start | bytes 393224 | tf_op jit(solution)/shard_map/while/body/eval_jaxpr/ppermute | solution.py:25
  248.1 8.7 %collective-permute-start.2 = (f32[8,2,16,256]{3,2,0,1:T(8,128)S(1)}, f32[8,2,16,256]{3,2,0,1:T(8,128)S(1)}, u32[]{:S(2)}, u32[]{:S(2)}) collective-permute-start(f32[8,2,16,256]{3,2,0,1:T(8,128)S(1)} %get-tuple-element.252), channel_id=1, source_target_pairs={{0,1},{1,2},{2,3},{3,4},{4,5},{5,6},{6,7},{8,9},{9,10},{10,11},{11... | collective-permute-start | bytes 786440 | tf_op jit(solution)/shard_map/while/body/eval_jaxpr/ppermute | solution.py:35
  257.6 12.6 %collective-permute-start = (f32[8,2,8,256]{3,2,0,1:T(8,128)}, f32[8,2,8,256]{3,2,0,1:T(8,128)}, u32[]{:S(2)}, u32[]{:S(2)}) collective-permute-start(f32[8,2,8,256]{3,2,0,1:T(8,128)} %get-tuple-element.217), channel_id=1, source_target_pairs={{0,8},{8,16},{16,24},{24,32},{32,40},{40,48},{48,56},{56,64},{64,7... | collective-permute-start | bytes 393224 | tf_op jit(solution)/shard_map/while/body/eval_jaxpr/ppermute | solution.py:23
  259.5 12.6 %collective-permute-start.1 = (f32[8,2,8,256]{3,2,0,1:T(8,128)}, f32[8,2,8,256]{3,2,0,1:T(8,128)}, u32[]{:S(2)}, u32[]{:S(2)}) collective-permute-start(f32[8,2,8,256]{3,2,0,1:T(8,128)} %get-tuple-element.218), channel_id=1, source_target_pairs={{8,0},{16,8},{24,16},{32,24},{40,32},{48,40},{56,48},{64,56},{72,6... | collective-permute-start | bytes 393224 | tf_op jit(solution)/shard_map/while/body/eval_jaxpr/ppermute | solution.py:25
  280.3 9.0 %collective-permute-start.2 = (f32[8,2,16,256]{3,2,0,1:T(8,128)S(1)}, f32[8,2,16,256]{3,2,0,1:T(8,128)S(1)}, u32[]{:S(2)}, u32[]{:S(2)}) collective-permute-start(f32[8,2,16,256]{3,2,0,1:T(8,128)S(1)} %get-tuple-element.252), channel_id=1, source_target_pairs={{0,1},{1,2},{2,3},{3,4},{4,5},{5,6},{6,7},{8,9},{9,10},{10,11},{11... | collective-permute-start | bytes 786440 | tf_op jit(solution)/shard_map/while/body/eval_jaxpr/ppermute | solution.py:35
  305.9 11.9 %copy-start.9 = (f32[8,16,256]{2,1,0:T(8,128)S(1)}, f32[8,16,256]{2,1,0:T(8,128)}, u32[]{:S(2)}) copy-start(f32[8,16,256]{2,1,0:T(8,128)} %param.10) | copy-start | bytes 393220
  (68 other events, 249.1 us)
Sparse Core Ops, SparseCore 0:
  317.9 43.5 reduce-scatter.3
where the time goes:
time: 438 us; the launch traced here: 435 us
  starting transfers between devices  131 us (30%)
  local copies, waits for them, and re-layouts  107 us (24%)
  other arithmetic  69.3 us (16%)
  waiting for transfers between devices  59.8 us (14%)
  blocking collectives  45.2 us (10%)
  between operations  14.3 us (3%)
  matrix products  5.26 us (1%)
    ppermute x9, starting transfers between devices, extended_2(): lax.ppermute(head, axis, [((i + 1) % count, i) for i in range(ends)])  57.3 us
    ppermute x8, starting transfers between devices, shifted(): return lax.ppermute(block, axis, route)  53.7 us
    add x64, other arithmetic, sweep(): attenuation * ((1.0 - TILT_SHARE) * intensity + TILT_SHARE * upwind)  51.4 us
    all_gather x1, blocking collectives, per_device(): lax.all_gather(populations_share, 'band', axis=3, tiled=True)  45.2 us
    unnamed x29, local copies, waits for them, and re-layouts  43.1 us
    unnamed x2, waiting for transfers between devices  43 us
    while x200, local copies, waits for them, and re-layouts  35.4 us
    ppermute x9, starting transfers between devices, extended_2(): lax.ppermute(tail, axis, [(i, (i + 1) % count) for i in range(ends)])  19.6 us
  transfers between devices with their start and end apart: 27, of which 11 were waited for; matrix products, arithmetic and copies ran while one was open for 12% of the time, Pallas kernels for 0%

commit v1 on v0

--- a/solution.py
+++ b/solution.py
@@ -121,7 +121,9 @@
     jbar_share = lax.psum_scatter(jbar, "band", scatter_dimension=3, tiled=True)
     planck_share = lax.dynamic_slice_in_dim(planck, offset, share, 2)
     populations_share = relax(jbar_share, planck_share)
-    populations_all = lax.all_gather(populations_share, "band", axis=3, tiled=True)
+    populations_all = jnp.concatenate(
+        lax.all_to_all(jnp.stack([populations_share] * lax.axis_size("band")), "band", 0, 0), axis=3
+    )
     new_source = EPS_THERMAL * planck[None] + (1.0 - EPS_THERMAL) * jnp.einsum(
         "ft,tzxy->fzxy", onehot, line_sources(populations_all), precision=highest
     )

time: 438 us -> 407 us (0.929)
  blocking collectives: 45.2 us -> 0 us
  waiting for transfers between devices: 59.8 us -> 70.4 us
    all_gather x1 -> x0, blocking collectives: 45.2 us -> none  [per_device(): lax.all_gather(populations_share, 'band', axis=3, tiled=True)]
    all_to_all x0 -> x1, waiting for transfers between devices: none -> 9.91 us  [per_device(): lax.all_to_all(jnp.stack([populations_share] * lax.axis_size('band')), 'b...]
    unnamed x29 -> x26, local copies, waits for them, and re-layouts: 43.1 us -> 40.5 us
  transfers between devices with their start and end apart: 27 -> 28, of which waited for: 11 -> 12; matrix products, arithmetic and copies ran while one was open for 12% -> 13% of each run, Pallas kernels for 0% -> 0%
where the time goes in v1:
time: 407 us; the launch traced here: 404 us
  starting transfers between devices  134 us (33%)
  local copies, waits for them, and re-layouts  105 us (26%)
  other arithmetic  71.1 us (17%)
  waiting for transfers between devices  70.4 us (17%)
  between operations  14.4 us (4%)
  matrix products  5.26 us (1%)
    ppermute x9, starting transfers between devices, extended_2(): lax.ppermute(head, axis, [((i + 1) % count, i) for i in range(ends)])  57.3 us
    ppermute x8, starting transfers between devices, shifted(): return lax.ppermute(block, axis, route)  53.7 us
    add x64, other arithmetic, sweep(): attenuation * ((1.0 - TILT_SHARE) * intensity + TILT_SHARE * upwind)  51.4 us
    unnamed x2, waiting for transfers between devices  43.6 us
    unnamed x26, local copies, waits for them, and re-layouts  40.5 us
    while x200, local copies, waits for them, and re-layouts  35.4 us
    ppermute x9, starting transfers between devices, extended_2(): lax.ppermute(tail, axis, [(i, (i + 1) % count) for i in range(ends)])  19.6 us
    all_to_all x1, waiting for transfers between devices, per_device(): lax.all_to_all(jnp.stack([populations_share] * lax.axis_size('band')), 'b...  9.91 us
  transfers between devices with their start and end apart: 28, of which 12 were waited for; matrix products, arithmetic and copies ran while one was open for 13% of the time, Pallas kernels for 0%

profile of v1, /device:TPU:8, one launch (start us, length us, event | category | flops | bytes accessed | tf_op | source)
XLA Modules:
  0.0 404.1 jit_solution(13068347927799107739)
XLA Ops:
  8.7 4.3 %collective-permute-start.3 = (f32[7,8,8,256]{3,2,1,0:T(8,128)S(1)}, f32[7,8,8,256]{3,2,1,0:T(8,128)S(1)}, u32[]{:S(2)}, u32[]{:S(2)}) collective-permute-start(f32[7,8,8,256]{3,2,1,0:T(8,128)S(1)} %get-tuple-element.112), channel_id=1, source_target_pairs={{0,8},{8,16},{16,24},{24,32},{32,40},{40,48},{48,56},{56,64},{64,7... | collective-permute-start | bytes 1376264 | tf_op jit(solution)/shard_map/ppermute | solution.py:23
  13.0 8.5 %collective-permute-start.4 = (f32[7,8,8,256]{3,2,1,0:T(8,128)S(1)}, f32[7,8,8,256]{3,2,1,0:T(8,128)}, u32[]{:S(2)}, u32[]{:S(2)}) collective-permute-start(f32[7,8,8,256]{3,2,1,0:T(8,128)S(1)} %get-tuple-element.113), channel_id=1, source_target_pairs={{8,0},{16,8},{24,16},{32,24},{40,32},{48,40},{56,48},{64,56},{72,6... | collective-permute-start | bytes 1376264 | tf_op jit(solution)/shard_map/ppermute | solution.py:25
  21.5 8.5 %collective-permute-done.3 = f32[7,8,8,256]{3,2,1,0:T(8,128)S(1)} collective-permute-done((f32[7,8,8,256]{3,2,1,0:T(8,128)S(1)}, f32[7,8,8,256]{3,2,1,0:T(8,128)S(1)}, u32[]{:S(2)}, u32[]{:S(2)}) %collective-permute-start.3) | collective-permute-done | bytes 458784 | tf_op jit(solution)/shard_map/ppermute | solution.py:23
  37.5 251.9 %while.12 = (s32[]{:T(128)}, f32[8,2,16,256]{3,2,0,1:T(8,128)S(1)}, f32[8,8,16,256]{3,2,0,1:T(8,128)}, f32[8]{0:T(128)S(1)}, f32[8,32,256]{2,1,0:T(8,128)S(1)}, /*index=5*/f32[8,8,32,256]{3,2,0,1:T(8,128)}, s32[]{:T(128)}) while((s32[]{:T(128)}, f32[8,2,16,256]{3,2,0,1:T(8,128)S(1)}, f32[8,8,16,256]{3,2,0,1:T(8,128)}, f32[8]{0:T(128)S(1)}, ...), condition=%wide.region_9.10_spmd, body=%wide.region_0.9_spmd.sunk | while | flops 24772616 | bytes 81658408 | solution.py:117
  40.5 6.6 %collective-permute-start.1 = (f32[8,2,8,256]{3,2,0,1:T(8,128)}, f32[8,2,8,256]{3,2,0,1:T(8,128)}, u32[]{:S(2)}, u32[]{:S(2)}) collective-permute-start(f32[8,2,8,256]{3,2,0,1:T(8,128)} %get-tuple-element.218), channel_id=1, source_target_pairs={{8,0},{16,8},{24,16},{32,24},{40,32},{48,40},{56,48},{64,56},{72,6... | collective-permute-start | bytes 393224 | tf_op jit(solution)/shard_map/while/body/eval_jaxpr/ppermute | solution.py:25
  47.1 2.8 multiply_bitcast_fusion.9
  67.0 6.0 %collective-permute-start.1 = (f32[8,2,8,256]{3,2,0,1:T(8,128)}, f32[8,2,8,256]{3,2,0,1:T(8,128)}, u32[]{:S(2)}, u32[]{:S(2)}) collective-permute-start(f32[8,2,8,256]{3,2,0,1:T(8,128)} %get-tuple-element.218), channel_id=1, source_target_pairs={{8,0},{16,8},{24,16},{32,24},{40,32},{48,40},{56,48},{64,56},{72,6... | collective-permute-start | bytes 393224 | tf_op jit(solution)/shard_map/while/body/eval_jaxpr/ppermute | solution.py:25
  73.1 2.8 multiply_bitcast_fusion.9
  87.9 6.8 %collective-permute-start.2 = (f32[8,2,16,256]{3,2,0,1:T(8,128)S(1)}, f32[8,2,16,256]{3,2,0,1:T(8,128)S(1)}, u32[]{:S(2)}, u32[]{:S(2)}) collective-permute-start(f32[8,2,16,256]{3,2,0,1:T(8,128)S(1)} %get-tuple-element.252), channel_id=1, source_target_pairs={{0,1},{1,2},{2,3},{3,4},{4,5},{5,6},{6,7},{8,9},{9,10},{10,11},{11... | collective-permute-start | bytes 786440 | tf_op jit(solution)/shard_map/while/body/eval_jaxpr/ppermute | solution.py:35
  98.5 6.0 %collective-permute-start.1 = (f32[8,2,8,256]{3,2,0,1:T(8,128)}, f32[8,2,8,256]{3,2,0,1:T(8,128)}, u32[]{:S(2)}, u32[]{:S(2)}) collective-permute-start(f32[8,2,8,256]{3,2,0,1:T(8,128)} %get-tuple-element.218), channel_id=1, source_target_pairs={{8,0},{16,8},{24,16},{32,24},{40,32},{48,40},{56,48},{64,56},{72,6... | collective-permute-start | bytes 393224 | tf_op jit(solution)/shard_map/while/body/eval_jaxpr/ppermute | solution.py:25
  104.6 2.8 multiply_bitcast_fusion.9
  119.4 7.5 %collective-permute-start.2 = (f32[8,2,16,256]{3,2,0,1:T(8,128)S(1)}, f32[8,2,16,256]{3,2,0,1:T(8,128)S(1)}, u32[]{:S(2)}, u32[]{:S(2)}) collective-permute-start(f32[8,2,16,256]{3,2,0,1:T(8,128)S(1)} %get-tuple-element.252), channel_id=1, source_target_pairs={{0,1},{1,2},{2,3},{3,4},{4,5},{5,6},{6,7},{8,9},{9,10},{10,11},{11... | collective-permute-start | bytes 786440 | tf_op jit(solution)/shard_map/while/body/eval_jaxpr/ppermute | solution.py:35
  130.7 6.0 %collective-permute-start.1 = (f32[8,2,8,256]{3,2,0,1:T(8,128)}, f32[8,2,8,256]{3,2,0,1:T(8,128)}, u32[]{:S(2)}, u32[]{:S(2)}) collective-permute-start(f32[8,2,8,256]{3,2,0,1:T(8,128)} %get-tuple-element.218), channel_id=1, source_target_pairs={{8,0},{16,8},{24,16},{32,24},{40,32},{48,40},{56,48},{64,56},{72,6... | collective-permute-start | bytes 393224 | tf_op jit(solution)/shard_map/while/body/eval_jaxpr/ppermute | solution.py:25
  136.8 2.8 multiply_bitcast_fusion.9
  151.5 7.6 %collective-permute-start.2 = (f32[8,2,16,256]{3,2,0,1:T(8,128)S(1)}, f32[8,2,16,256]{3,2,0,1:T(8,128)S(1)}, u32[]{:S(2)}, u32[]{:S(2)}) collective-permute-start(f32[8,2,16,256]{3,2,0,1:T(8,128)S(1)} %get-tuple-element.252), channel_id=1, source_target_pairs={{0,1},{1,2},{2,3},{3,4},{4,5},{5,6},{6,7},{8,9},{9,10},{10,11},{11... | collective-permute-start | bytes 786440 | tf_op jit(solution)/shard_map/while/body/eval_jaxpr/ppermute | solution.py:35
  162.9 6.0 %collective-permute-start.1 = (f32[8,2,8,256]{3,2,0,1:T(8,128)}, f32[8,2,8,256]{3,2,0,1:T(8,128)}, u32[]{:S(2)}, u32[]{:S(2)}) collective-permute-start(f32[8,2,8,256]{3,2,0,1:T(8,128)} %get-tuple-element.218), channel_id=1, source_target_pairs={{8,0},{16,8},{24,16},{32,24},{40,32},{48,40},{56,48},{64,56},{72,6... | collective-permute-start | bytes 393224 | tf_op jit(solution)/shard_map/while/body/eval_jaxpr/ppermute | solution.py:25
  169.0 2.8 multiply_bitcast_fusion.9
  183.8 7.6 %collective-permute-start.2 = (f32[8,2,16,256]{3,2,0,1:T(8,128)S(1)}, f32[8,2,16,256]{3,2,0,1:T(8,128)S(1)}, u32[]{:S(2)}, u32[]{:S(2)}) collective-permute-start(f32[8,2,16,256]{3,2,0,1:T(8,128)S(1)} %get-tuple-element.252), channel_id=1, source_target_pairs={{0,1},{1,2},{2,3},{3,4},{4,5},{5,6},{6,7},{8,9},{9,10},{10,11},{11... | collective-permute-start | bytes 786440 | tf_op jit(solution)/shard_map/while/body/eval_jaxpr/ppermute | solution.py:35
  195.2 6.0 %collective-permute-start.1 = (f32[8,2,8,256]{3,2,0,1:T(8,128)}, f32[8,2,8,256]{3,2,0,1:T(8,128)}, u32[]{:S(2)}, u32[]{:S(2)}) collective-permute-start(f32[8,2,8,256]{3,2,0,1:T(8,128)} %get-tuple-element.218), channel_id=1, source_target_pairs={{8,0},{16,8},{24,16},{32,24},{40,32},{48,40},{56,48},{64,56},{72,6... | collective-permute-start | bytes 393224 | tf_op jit(solution)/shard_map/while/body/eval_jaxpr/ppermute | solution.py:25
  216.0 7.6 %collective-permute-start.2 = (f32[8,2,16,256]{3,2,0,1:T(8,128)S(1)}, f32[8,2,16,256]{3,2,0,1:T(8,128)S(1)}, u32[]{:S(2)}, u32[]{:S(2)}) collective-permute-start(f32[8,2,16,256]{3,2,0,1:T(8,128)S(1)} %get-tuple-element.252), channel_id=1, source_target_pairs={{0,1},{1,2},{2,3},{3,4},{4,5},{5,6},{6,7},{8,9},{9,10},{10,11},{11... | collective-permute-start | bytes 786440 | tf_op jit(solution)/shard_map/while/body/eval_jaxpr/ppermute | solution.py:35
  227.4 6.0 %collective-permute-start.1 = (f32[8,2,8,256]{3,2,0,1:T(8,128)}, f32[8,2,8,256]{3,2,0,1:T(8,128)}, u32[]{:S(2)}, u32[]{:S(2)}) collective-permute-start(f32[8,2,8,256]{3,2,0,1:T(8,128)} %get-tuple-element.218), channel_id=1, source_target_pairs={{8,0},{16,8},{24,16},{32,24},{40,32},{48,40},{56,48},{64,56},{72,6... | collective-permute-start | bytes 393224 | tf_op jit(solution)/shard_map/while/body/eval_jaxpr/ppermute | solution.py:25
  248.3 7.6 %collective-permute-start.2 = (f32[8,2,16,256]{3,2,0,1:T(8,128)S(1)}, f32[8,2,16,256]{3,2,0,1:T(8,128)S(1)}, u32[]{:S(2)}, u32[]{:S(2)}) collective-permute-start(f32[8,2,16,256]{3,2,0,1:T(8,128)S(1)} %get-tuple-element.252), channel_id=1, source_target_pairs={{0,1},{1,2},{2,3},{3,4},{4,5},{5,6},{6,7},{8,9},{9,10},{10,11},{11... | collective-permute-start | bytes 786440 | tf_op jit(solution)/shard_map/while/body/eval_jaxpr/ppermute | solution.py:35
  259.7 6.0 %collective-permute-start.1 = (f32[8,2,8,256]{3,2,0,1:T(8,128)}, f32[8,2,8,256]{3,2,0,1:T(8,128)}, u32[]{:S(2)}, u32[]{:S(2)}) collective-permute-start(f32[8,2,8,256]{3,2,0,1:T(8,128)} %get-tuple-element.218), channel_id=1, source_target_pairs={{8,0},{16,8},{24,16},{32,24},{40,32},{48,40},{56,48},{64,56},{72,6... | collective-permute-start | bytes 393224 | tf_op jit(solution)/shard_map/while/body/eval_jaxpr/ppermute | solution.py:25
  280.5 7.8 %collective-permute-start.2 = (f32[8,2,16,256]{3,2,0,1:T(8,128)S(1)}, f32[8,2,16,256]{3,2,0,1:T(8,128)S(1)}, u32[]{:S(2)}, u32[]{:S(2)}) collective-permute-start(f32[8,2,16,256]{3,2,0,1:T(8,128)S(1)} %get-tuple-element.252), channel_id=1, source_target_pairs={{0,1},{1,2},{2,3},{3,4},{4,5},{5,6},{6,7},{8,9},{9,10},{10,11},{11... | collective-permute-start | bytes 786440 | tf_op jit(solution)/shard_map/while/body/eval_jaxpr/ppermute | solution.py:35
  289.5 2.8 fusion.33
  292.3 13.8 %copy.28 = f32[5,8,16,256]{0,2,1,3:T(8,128)} copy(f32[5,8,16,256]{3,0,2,1:T(8,128)S(1)} %fusion.33) | data formatting | bytes 1310720
  306.1 11.9 %reshape.263 = f32[256,640]{1,0:T(8,128)} reshape(f32[256,8,16,5]{3,2,1,0:T(8,128)} %bitcast.212) | data formatting | bytes 1310720
  318.1 43.6 %reduce-scatter.4.cloned.1.call-done = f32[64,640]{1,0:T(8,128)} async-done(((f32[256,640]{1,0:T(8,128)}), f32[64,640]{1,0:T(8,128)}) %reduce-scatter.4.cloned.1.call-update) | async-done | bytes 163856
  361.7 6.2 %reshape.264 = f32[64,8,16,5]{3,2,1,0:T(8,128)} reshape(f32[64,640]{1,0:T(8,128)} %reduce-scatter.4.cloned.1.call-done) | data formatting | bytes 327680
  368.0 3.8 copy.29
  374.7 3.5 all-to-all-start
  378.2 9.9 %all-to-all-done = f32[4,1,40960]{2,1,0:T(1,128)S(1)} async-done(((f32[4,1,40960]{2,1,0:T(1,128)}), f32[4,1,40960]{2,1,0:T(1,128)S(1)}, u32[]{:S(2)}, u32[]{:S(2)}) %all-to-all-start) | async-done | bytes 655392 | tf_op jit(solution)/shard_map/all_to_all | solution.py:125
  (656 shorter events, 154.1 us)
Async XLA Ops:
  7.2 354.6 %reduce-scatter.4.cloned.1.call-start = ((), (), s32[]{:S(2)}) async-start(), calls=%async_computation.2 | async-start | bytes 819200
  7.2 24.0 %copy-start.7 = (f32[5,8,16,256]{3,2,1,0:T(8,128)S(1)}, f32[5,8,16,256]{3,2,1,0:T(8,128)}, u32[]{:S(2)}) copy-start(f32[5,8,16,256]{3,2,1,0:T(8,128)} %param.11) | copy-start | bytes 1966084
  7.2 24.0 %copy-start.8 = (f32[8,16,256]{2,1,0:T(8,128)S(1)}, f32[8,16,256]{2,1,0:T(8,128)}, u32[]{:S(2)}) copy-start(f32[8,16,256]{2,1,0:T(8,128)} %param.10) | copy-start | bytes 393220
  7.2 24.0 %copy-start.12 = (f32[8,16,256]{2,1,0:T(8,128)S(1)}, f32[8,16,256]{2,1,0:T(8,128)}, u32[]{:S(2)}) copy-start(f32[8,16,256]{2,1,0:T(8,128)} %param.9) | copy-start | bytes 393220
  8.7 21.3 %collective-permute-start.3 = (f32[7,8,8,256]{3,2,1,0:T(8,128)S(1)}, f32[7,8,8,256]{3,2,1,0:T(8,128)S(1)}, u32[]{:S(2)}, u32[]{:S(2)}) collective-permute-start(f32[7,8,8,256]{3,2,1,0:T(8,128)S(1)} %get-tuple-element.112), channel_id=1, source_target_pairs={{0,8},{8,16},{16,24},{24,32},{32,40},{40,48},{48,56},{56,64},{64,7... | collective-permute-start | bytes 1376264 | tf_op jit(solution)/shard_map/ppermute | solution.py:23
  13.0 18.2 %collective-permute-start.4 = (f32[7,8,8,256]{3,2,1,0:T(8,128)S(1)}, f32[7,8,8,256]{3,2,1,0:T(8,128)}, u32[]{:S(2)}, u32[]{:S(2)}) collective-permute-start(f32[7,8,8,256]{3,2,1,0:T(8,128)S(1)} %get-tuple-element.113), channel_id=1, source_target_pairs={{8,0},{16,8},{24,16},{32,24},{40,32},{48,40},{56,48},{64,56},{72,6... | collective-permute-start | bytes 1376264 | tf_op jit(solution)/shard_map/ppermute | solution.py:25
  37.5 251.9 %copy-start.15 = (f32[8]{0:T(128)S(1)}, f32[8]{0:T(128)}, u32[]{:S(2)}) copy-start(f32[8]{0:T(128)} %param.13) | copy-start | bytes 100
  38.5 13.2 %collective-permute-start = (f32[8,2,8,256]{3,2,0,1:T(8,128)}, f32[8,2,8,256]{3,2,0,1:T(8,128)}, u32[]{:S(2)}, u32[]{:S(2)}) collective-permute-start(f32[8,2,8,256]{3,2,0,1:T(8,128)} %get-tuple-element.217), channel_id=1, source_target_pairs={{0,8},{8,16},{16,24},{24,32},{32,40},{40,48},{48,56},{56,64},{64,7... | collective-permute-start | bytes 393224 | tf_op jit(solution)/shard_map/while/body/eval_jaxpr/ppermute | solution.py:23
  40.5 13.2 %collective-permute-start.1 = (f32[8,2,8,256]{3,2,0,1:T(8,128)}, f32[8,2,8,256]{3,2,0,1:T(8,128)}, u32[]{:S(2)}, u32[]{:S(2)}) collective-permute-start(f32[8,2,8,256]{3,2,0,1:T(8,128)} %get-tuple-element.218), channel_id=1, source_target_pairs={{8,0},{16,8},{24,16},{32,24},{40,32},{48,40},{56,48},{64,56},{72,6... | collective-permute-start | bytes 393224 | tf_op jit(solution)/shard_map/while/body/eval_jaxpr/ppermute | solution.py:25
  61.9 2.4 collective-permute-start.2
  65.1 12.6 %collective-permute-start = (f32[8,2,8,256]{3,2,0,1:T(8,128)}, f32[8,2,8,256]{3,2,0,1:T(8,128)}, u32[]{:S(2)}, u32[]{:S(2)}) collective-permute-start(f32[8,2,8,256]{3,2,0,1:T(8,128)} %get-tuple-element.217), channel_id=1, source_target_pairs={{0,8},{8,16},{16,24},{24,32},{32,40},{40,48},{48,56},{56,64},{64,7... | collective-permute-start | bytes 393224 | tf_op jit(solution)/shard_map/while/body/eval_jaxpr/ppermute | solution.py:23
  67.0 12.6 %collective-permute-start.1 = (f32[8,2,8,256]{3,2,0,1:T(8,128)}, f32[8,2,8,256]{3,2,0,1:T(8,128)}, u32[]{:S(2)}, u32[]{:S(2)}) collective-permute-start(f32[8,2,8,256]{3,2,0,1:T(8,128)} %get-tuple-element.218), channel_id=1, source_target_pairs={{8,0},{16,8},{24,16},{32,24},{40,32},{48,40},{56,48},{64,56},{72,6... | collective-permute-start | bytes 393224 | tf_op jit(solution)/shard_map/while/body/eval_jaxpr/ppermute | solution.py:25
  87.9 8.0 %collective-permute-start.2 = (f32[8,2,16,256]{3,2,0,1:T(8,128)S(1)}, f32[8,2,16,256]{3,2,0,1:T(8,128)S(1)}, u32[]{:S(2)}, u32[]{:S(2)}) collective-permute-start(f32[8,2,16,256]{3,2,0,1:T(8,128)S(1)} %get-tuple-element.252), channel_id=1, source_target_pairs={{0,1},{1,2},{2,3},{3,4},{4,5},{5,6},{6,7},{8,9},{9,10},{10,11},{11... | collective-permute-start | bytes 786440 | tf_op jit(solution)/shard_map/while/body/eval_jaxpr/ppermute | solution.py:35
  96.6 12.6 %collective-permute-start = (f32[8,2,8,256]{3,2,0,1:T(8,128)}, f32[8,2,8,256]{3,2,0,1:T(8,128)}, u32[]{:S(2)}, u32[]{:S(2)}) collective-permute-start(f32[8,2,8,256]{3,2,0,1:T(8,128)} %get-tuple-element.217), channel_id=1, source_target_pairs={{0,8},{8,16},{16,24},{24,32},{32,40},{40,48},{48,56},{56,64},{64,7... | collective-permute-start | bytes 393224 | tf_op jit(solution)/shard_map/while/body/eval_jaxpr/ppermute | solution.py:23
  98.5 12.6 %collective-permute-start.1 = (f32[8,2,8,256]{3,2,0,1:T(8,128)}, f32[8,2,8,256]{3,2,0,1:T(8,128)}, u32[]{:S(2)}, u32[]{:S(2)}) collective-permute-start(f32[8,2,8,256]{3,2,0,1:T(8,128)} %get-tuple-element.218), channel_id=1, source_target_pairs={{8,0},{16,8},{24,16},{32,24},{40,32},{48,40},{56,48},{64,56},{72,6... | collective-permute-start | bytes 393224 | tf_op jit(solution)/shard_map/while/body/eval_jaxpr/ppermute | solution.py:25
  119.4 8.6 %collective-permute-start.2 = (f32[8,2,16,256]{3,2,0,1:T(8,128)S(1)}, f32[8,2,16,256]{3,2,0,1:T(8,128)S(1)}, u32[]{:S(2)}, u32[]{:S(2)}) collective-permute-start(f32[8,2,16,256]{3,2,0,1:T(8,128)S(1)} %get-tuple-element.252), channel_id=1, source_target_pairs={{0,1},{1,2},{2,3},{3,4},{4,5},{5,6},{6,7},{8,9},{9,10},{10,11},{11... | collective-permute-start | bytes 786440 | tf_op jit(solution)/shard_map/while/body/eval_jaxpr/ppermute | solution.py:35
  128.8 12.6 %collective-permute-start = (f32[8,2,8,256]{3,2,0,1:T(8,128)}, f32[8,2,8,256]{3,2,0,1:T(8,128)}, u32[]{:S(2)}, u32[]{:S(2)}) collective-permute-start(f32[8,2,8,256]{3,2,0,1:T(8,128)} %get-tuple-element.217), channel_id=1, source_target_pairs={{0,8},{8,16},{16,24},{24,32},{32,40},{40,48},{48,56},{56,64},{64,7... | collective-permute-start | bytes 393224 | tf_op jit(solution)/shard_map/while/body/eval_jaxpr/ppermute | solution.py:23
  130.7 12.6 %collective-permute-start.1 = (f32[8,2,8,256]{3,2,0,1:T(8,128)}, f32[8,2,8,256]{3,2,0,1:T(8,128)}, u32[]{:S(2)}, u32[]{:S(2)}) collective-permute-start(f32[8,2,8,256]{3,2,0,1:T(8,128)} %get-tuple-element.218), channel_id=1, source_target_pairs={{8,0},{16,8},{24,16},{32,24},{40,32},{48,40},{56,48},{64,56},{72,6... | collective-permute-start | bytes 393224 | tf_op jit(solution)/shard_map/while/body/eval_jaxpr/ppermute | solution.py:25
  151.5 8.7 %collective-permute-start.2 = (f32[8,2,16,256]{3,2,0,1:T(8,128)S(1)}, f32[8,2,16,256]{3,2,0,1:T(8,128)S(1)}, u32[]{:S(2)}, u32[]{:S(2)}) collective-permute-start(f32[8,2,16,256]{3,2,0,1:T(8,128)S(1)} %get-tuple-element.252), channel_id=1, source_target_pairs={{0,1},{1,2},{2,3},{3,4},{4,5},{5,6},{6,7},{8,9},{9,10},{10,11},{11... | collective-permute-start | bytes 786440 | tf_op jit(solution)/shard_map/while/body/eval_jaxpr/ppermute | solution.py:35
  161.0 12.6 %collective-permute-start = (f32[8,2,8,256]{3,2,0,1:T(8,128)}, f32[8,2,8,256]{3,2,0,1:T(8,128)}, u32[]{:S(2)}, u32[]{:S(2)}) collective-permute-start(f32[8,2,8,256]{3,2,0,1:T(8,128)} %get-tuple-element.217), channel_id=1, source_target_pairs={{0,8},{8,16},{16,24},{24,32},{32,40},{40,48},{48,56},{56,64},{64,7... | collective-permute-start | bytes 393224 | tf_op jit(solution)/shard_map/while/body/eval_jaxpr/ppermute | solution.py:23
  162.9 12.6 %collective-permute-start.1 = (f32[8,2,8,256]{3,2,0,1:T(8,128)}, f32[8,2,8,256]{3,2,0,1:T(8,128)}, u32[]{:S(2)}, u32[]{:S(2)}) collective-permute-start(f32[8,2,8,256]{3,2,0,1:T(8,128)} %get-tuple-element.218), channel_id=1, source_target_pairs={{8,0},{16,8},{24,16},{32,24},{40,32},{48,40},{56,48},{64,56},{72,6... | collective-permute-start | bytes 393224 | tf_op jit(solution)/shard_map/while/body/eval_jaxpr/ppermute | solution.py:25
  183.8 8.7 %collective-permute-start.2 = (f32[8,2,16,256]{3,2,0,1:T(8,128)S(1)}, f32[8,2,16,256]{3,2,0,1:T(8,128)S(1)}, u32[]{:S(2)}, u32[]{:S(2)}) collective-permute-start(f32[8,2,16,256]{3,2,0,1:T(8,128)S(1)} %get-tuple-element.252), channel_id=1, source_target_pairs={{0,1},{1,2},{2,3},{3,4},{4,5},{5,6},{6,7},{8,9},{9,10},{10,11},{11... | collective-permute-start | bytes 786440 | tf_op jit(solution)/shard_map/while/body/eval_jaxpr/ppermute | solution.py:35
  193.3 12.6 %collective-permute-start = (f32[8,2,8,256]{3,2,0,1:T(8,128)}, f32[8,2,8,256]{3,2,0,1:T(8,128)}, u32[]{:S(2)}, u32[]{:S(2)}) collective-permute-start(f32[8,2,8,256]{3,2,0,1:T(8,128)} %get-tuple-element.217), channel_id=1, source_target_pairs={{0,8},{8,16},{16,24},{24,32},{32,40},{40,48},{48,56},{56,64},{64,7... | collective-permute-start | bytes 393224 | tf_op jit(solution)/shard_map/while/body/eval_jaxpr/ppermute | solution.py:23
  195.2 12.6 %collective-permute-start.1 = (f32[8,2,8,256]{3,2,0,1:T(8,128)}, f32[8,2,8,256]{3,2,0,1:T(8,128)}, u32[]{:S(2)}, u32[]{:S(2)}) collective-permute-start(f32[8,2,8,256]{3,2,0,1:T(8,128)} %get-tuple-element.218), channel_id=1, source_target_pairs={{8,0},{16,8},{24,16},{32,24},{40,32},{48,40},{56,48},{64,56},{72,6... | collective-permute-start | bytes 393224 | tf_op jit(solution)/shard_map/while/body/eval_jaxpr/ppermute | solution.py:25
  216.0 8.7 %collective-permute-start.2 = (f32[8,2,16,256]{3,2,0,1:T(8,128)S(1)}, f32[8,2,16,256]{3,2,0,1:T(8,128)S(1)}, u32[]{:S(2)}, u32[]{:S(2)}) collective-permute-start(f32[8,2,16,256]{3,2,0,1:T(8,128)S(1)} %get-tuple-element.252), channel_id=1, source_target_pairs={{0,1},{1,2},{2,3},{3,4},{4,5},{5,6},{6,7},{8,9},{9,10},{10,11},{11... | collective-permute-start | bytes 786440 | tf_op jit(solution)/shard_map/while/body/eval_jaxpr/ppermute | solution.py:35
  225.5 12.6 %collective-permute-start = (f32[8,2,8,256]{3,2,0,1:T(8,128)}, f32[8,2,8,256]{3,2,0,1:T(8,128)}, u32[]{:S(2)}, u32[]{:S(2)}) collective-permute-start(f32[8,2,8,256]{3,2,0,1:T(8,128)} %get-tuple-element.217), channel_id=1, source_target_pairs={{0,8},{8,16},{16,24},{24,32},{32,40},{40,48},{48,56},{56,64},{64,7... | collective-permute-start | bytes 393224 | tf_op jit(solution)/shard_map/while/body/eval_jaxpr/ppermute | solution.py:23
  227.4 12.6 %collective-permute-start.1 = (f32[8,2,8,256]{3,2,0,1:T(8,128)}, f32[8,2,8,256]{3,2,0,1:T(8,128)}, u32[]{:S(2)}, u32[]{:S(2)}) collective-permute-start(f32[8,2,8,256]{3,2,0,1:T(8,128)} %get-tuple-element.218), channel_id=1, source_target_pairs={{8,0},{16,8},{24,16},{32,24},{40,32},{48,40},{56,48},{64,56},{72,6... | collective-permute-start | bytes 393224 | tf_op jit(solution)/shard_map/while/body/eval_jaxpr/ppermute | solution.py:25
  248.3 8.7 %collective-permute-start.2 = (f32[8,2,16,256]{3,2,0,1:T(8,128)S(1)}, f32[8,2,16,256]{3,2,0,1:T(8,128)S(1)}, u32[]{:S(2)}, u32[]{:S(2)}) collective-permute-start(f32[8,2,16,256]{3,2,0,1:T(8,128)S(1)} %get-tuple-element.252), channel_id=1, source_target_pairs={{0,1},{1,2},{2,3},{3,4},{4,5},{5,6},{6,7},{8,9},{9,10},{10,11},{11... | collective-permute-start | bytes 786440 | tf_op jit(solution)/shard_map/while/body/eval_jaxpr/ppermute | solution.py:35
  257.7 12.6 %collective-permute-start = (f32[8,2,8,256]{3,2,0,1:T(8,128)}, f32[8,2,8,256]{3,2,0,1:T(8,128)}, u32[]{:S(2)}, u32[]{:S(2)}) collective-permute-start(f32[8,2,8,256]{3,2,0,1:T(8,128)} %get-tuple-element.217), channel_id=1, source_target_pairs={{0,8},{8,16},{16,24},{24,32},{32,40},{40,48},{48,56},{56,64},{64,7... | collective-permute-start | bytes 393224 | tf_op jit(solution)/shard_map/while/body/eval_jaxpr/ppermute | solution.py:23
  259.7 12.6 %collective-permute-start.1 = (f32[8,2,8,256]{3,2,0,1:T(8,128)}, f32[8,2,8,256]{3,2,0,1:T(8,128)}, u32[]{:S(2)}, u32[]{:S(2)}) collective-permute-start(f32[8,2,8,256]{3,2,0,1:T(8,128)} %get-tuple-element.218), channel_id=1, source_target_pairs={{8,0},{16,8},{24,16},{32,24},{40,32},{48,40},{56,48},{64,56},{72,6... | collective-permute-start | bytes 393224 | tf_op jit(solution)/shard_map/while/body/eval_jaxpr/ppermute | solution.py:25
  280.5 9.0 %collective-permute-start.2 = (f32[8,2,16,256]{3,2,0,1:T(8,128)S(1)}, f32[8,2,16,256]{3,2,0,1:T(8,128)S(1)}, u32[]{:S(2)}, u32[]{:S(2)}) collective-permute-start(f32[8,2,16,256]{3,2,0,1:T(8,128)S(1)} %get-tuple-element.252), channel_id=1, source_target_pairs={{0,1},{1,2},{2,3},{3,4},{4,5},{5,6},{6,7},{8,9},{9,10},{10,11},{11... | collective-permute-start | bytes 786440 | tf_op jit(solution)/shard_map/while/body/eval_jaxpr/ppermute | solution.py:35
  374.7 13.4 %all-to-all-start = ((f32[4,1,40960]{2,1,0:T(1,128)}), f32[4,1,40960]{2,1,0:T(1,128)S(1)}, u32[]{:S(2)}, u32[]{:S(2)}) async-start(f32[4,1,40960]{2,1,0:T(1,128)} %reshape.265), calls=%async_computation | async-start | bytes 1310720 | tf_op jit(solution)/shard_map/all_to_all | solution.py:125
  (69 other events, 261.3 us)
Sparse Core Ops, SparseCore 0:
  318.1 43.5 reduce-scatter.3
